TPU v7x, 256 devices: a whole 4x4x8 slice. The times are simulated.
256 devices in a mesh: ctx: 64 (over z, x, core), fsdp: 4 (over y).
Axes of the slice: x: 4, y: 4, z: 8, core: 2. Of those that a mesh axis runs over, the one named last changes fastest.
Arguments:
- queries: bfloat16 [8192, 2048], P('ctx', 'fsdp'), may hold values from -120 to 120
- keys: bfloat16 [8192, 256], P('ctx'), may hold values from -5 to 5
- values: bfloat16 [8192, 256], P('ctx'), may hold values from -5 to 5
- out_grad: bfloat16 [8192, 2048], P('ctx', 'fsdp'), may hold values from -5 to 5
- hidden: bfloat16 [8192, 8192], P('ctx', 'fsdp'), may hold values from -40 to 40
- key_weight: bfloat16 [8192, 256], P('fsdp'), may hold values from -10 to 10
- value_weight: bfloat16 [8192, 256], P('fsdp'), may hold values from -10 to 10
- stretch_owner: int32 [64], replicated, may hold values from 0 to 63, as said below
- positions: int32 [8192], P('ctx'), may hold values from 0 to 4095, as said below
Outputs:
- query_grad: bfloat16 [8192, 2048], P('ctx', 'fsdp')
- key_weight_grad: float32 [8192, 256], P('fsdp')
- value_weight_grad: float32 [8192, 256], P('fsdp')
Inputs may be any that keep to these rules, and one draw needn't show every extreme that they name: A permutation; index b of ctx holds sequence stretch stretch_owner[b] in its first 64 rows and stretch 2 * 64 - 1 - stretch_owner[b] in the others. `positions`: documents are contiguous in sequence order; a row's position counts from its document's first token, and the sequence's first token has position 0.
All inputs are finite; a program needn't handle non-finite values.
Results may differ from a plain program's by a relative error of at most 0.015.
Values may be sent and summed in bfloat16 or wider, within the bound.
A program may use at most 64 MiB of HBM per device.

v0:
```python
import math
import jax
import jax.numpy as jnp
from jax import lax
from jax.sharding import PartitionSpec as P

DH = 128
HPG = 8
KVG = 2
CLIP_RATE = 0.02
EPSILON = 1e-06
NEGATIVE = -1e30


def rows_by_head(block, heads, width):
    count = block.shape[0]
    return block.reshape(count, heads, width).transpose(1, 0, 2).reshape(heads * count, width)


def local(
    queries, keys, values, out_grad, hidden, key_weight, value_weight, stretch_owner, positions
):
    tok_dev = queries.shape[0]
    heads = queries.shape[1] // DH
    ctx_count = lax.axis_size("ctx")
    total = tok_dev * ctx_count
    half = tok_dev // 2
    ctx_index = lax.axis_index("ctx")
    group = lax.axis_index("fsdp") * heads // HPG
    scale = 1.0 / math.sqrt(DH)
    block = min(512, total)
    blocks = total // block
    query_count = heads * tok_dev
    own_keys = lax.dynamic_slice_in_dim(keys, group * DH, DH, 1)
    own_values = lax.dynamic_slice_in_dim(values, group * DH, DH, 1)
    all_keys, all_values = (
        lax.all_gather(own_keys, "ctx", axis=0, tiled=True),
        lax.all_gather(own_values, "ctx", axis=0, tiled=True),
    )
    offsets = jnp.arange(half, dtype=jnp.int32)
    stretches = jnp.stack([stretch_owner, 2 * ctx_count - 1 - stretch_owner], axis=1)
    key_place = (stretches[:, :, None] * half + offsets[None, None, :]).reshape(total)
    mine = lax.dynamic_slice_in_dim(stretches, ctx_index, 1, 0)[0]
    local_place = (mine[:, None] * half + offsets[None, :]).reshape(tok_dev)
    query_place = jnp.tile(local_place, heads)
    query_floor = jnp.tile(local_place - positions, heads)
    query_rows = rows_by_head(queries, heads, DH)
    grad_rows = rows_by_head(out_grad, heads, DH)
    contract_last = (((1,), (1,)), ((), ()))
    contract_first = (((0,), (0,)), ((), ()))

    def scores_at(start, width):
        key_block = lax.dynamic_slice_in_dim(all_keys, start, width, 0)
        place = lax.dynamic_slice_in_dim(key_place, start, width, 0)
        raw = (
            lax.dot_general(
                query_rows, key_block, contract_last, preferred_element_type=jnp.float32
            )
            * scale
        )
        seen = (place[None, :] <= query_place[:, None]) & (place[None, :] >= query_floor[:, None])
        return (jnp.where(seen, raw, NEGATIVE), seen, key_block)

    def stats_step(step, carry):
        top, mass = carry
        masked, seen, key_block = scores_at(step * block, block)
        new_top = jnp.maximum(top, jnp.max(masked, axis=1))
        weights = jnp.where(seen, jnp.exp(masked - new_top[:, None]), 0.0)
        mass = mass * jnp.exp(top - new_top) + jnp.sum(weights, axis=1)
        return (new_top, mass)

    start_top = jnp.full((query_count,), NEGATIVE, jnp.float32)
    start_mass = jnp.zeros((query_count,), jnp.float32)
    top, mass = lax.fori_loop(0, blocks, stats_step, (start_top, start_mass))
    lse = top + jnp.log(mass)

    def probs_at(start, width):
        masked, seen, key_block = scores_at(start, width)
        probs = jnp.where(seen, jnp.exp(masked - lse[:, None]), 0.0)
        value_block = lax.dynamic_slice_in_dim(all_values, start, width, 0)
        dprobs = lax.dot_general(
            grad_rows, value_block, contract_last, preferred_element_type=jnp.float32
        )
        return (probs, dprobs, key_block)

    def delta_step(step, acc):
        probs, dprobs, key_block = probs_at(step * block, block)
        return acc + jnp.sum(probs * dprobs, axis=1)

    delta = lax.fori_loop(0, blocks, delta_step, jnp.zeros((query_count,), jnp.float32))

    def slopes_at(start, width):
        probs, dprobs, key_block = probs_at(start, width)
        slopes = (probs * (dprobs - delta[:, None]) * scale).astype(jnp.bfloat16)
        return (probs.astype(jnp.bfloat16), slopes, key_block)

    def key_terms(probs_b, slopes):
        key_part = lax.dot_general(
            slopes, query_rows, contract_first, preferred_element_type=jnp.float32
        )
        value_part = lax.dot_general(
            probs_b, grad_rows, contract_first, preferred_element_type=jnp.float32
        )
        return jnp.concatenate([key_part, value_part], axis=1)

    start_query = jnp.zeros((query_count, DH), jnp.float32)

    def full_step(step, carry):
        query_acc, terms = carry
        start = step * block
        probs_b, slopes, key_block = slopes_at(start, block)
        query_acc = query_acc + jnp.dot(slopes, key_block, preferred_element_type=jnp.float32)
        terms = lax.dynamic_update_slice_in_dim(terms, key_terms(probs_b, slopes), start, 0)
        return (query_acc, terms)

    start_terms = jnp.zeros((total, 2 * DH), jnp.float32)
    query_acc, terms = lax.fori_loop(0, blocks, full_step, (start_query, start_terms))
    own_grads = lax.psum_scatter(terms, "ctx", scatter_dimension=0, tiled=True)
    query_grad = (
        query_acc.reshape(heads, tok_dev, DH)
        .transpose(1, 0, 2)
        .reshape(tok_dev, heads * DH)
        .astype(jnp.bfloat16)
    )
    members = lax.all_gather(own_grads.astype(jnp.bfloat16), "fsdp", axis=0, tiled=True).astype(
        own_grads.dtype
    )
    per_group = members.reshape(KVG, -1, tok_dev, 2 * DH).sum(axis=1)
    key_grads = (
        per_group[:, :, :DH].transpose(1, 0, 2).reshape(tok_dev, KVG * DH).astype(jnp.bfloat16)
    )
    value_grads = (
        per_group[:, :, DH:].transpose(1, 0, 2).reshape(tok_dev, KVG * DH).astype(jnp.bfloat16)
    )
    both_grads = jnp.concatenate([key_grads, value_grads], axis=1)
    columns = KVG * DH
    raw = lax.psum(
        lax.dot_general(hidden, both_grads, contract_first, preferred_element_type=jnp.float32),
        "ctx",
    )
    key_f = key_weight.astype(jnp.float32)
    value_f = value_weight.astype(jnp.float32)
    grad_sq, key_sq, value_sq = lax.psum(
        (
            jnp.sum(raw * raw, axis=0),
            jnp.sum(key_f * key_f, axis=0),
            jnp.sum(value_f * value_f, axis=0),
        ),
        "fsdp",
    )
    weight_norm = jnp.sqrt(jnp.concatenate([key_sq, value_sq]) + EPSILON)
    grad_norm = jnp.sqrt(grad_sq + EPSILON)
    clipped = raw * jnp.minimum(1.0, CLIP_RATE * total * weight_norm / grad_norm)[None, :]
    return (query_grad, clipped[:, :columns], clipped[:, columns:])


def solution(mesh):
    return jax.shard_map(
        local,
        mesh=mesh,
        in_specs=(
            P("ctx", "fsdp"),
            P("ctx", None),
            P("ctx", None),
            P("ctx", "fsdp"),
            P("ctx", "fsdp"),
            P("fsdp", None),
            P("fsdp", None),
            P(),
            P("ctx"),
        ),
        out_specs=(P("ctx", "fsdp"), P("fsdp", None), P("fsdp", None)),
        check_vma=False,
    )
```

profile of v0, /device:TPU:2, one launch (start us, length us, event | category | flops | bytes accessed | tf_op | source)
XLA Modules:
  0.0 693.1 jit_solution(3216926837924583909)
XLA Ops:
  7.2 1.4 constant_dynamic-slice_fusion.1
  8.7 1.4 constant_dynamic-slice_fusion
  14.8 75.9 %all-gather.3.cloned.1.call-done = bf16[8192,128]{1,0:T(8,128)(2,1)} async-done(((bf16[128,128]{1,0:T(8,128)(2,1)}), bf16[8192,128]{1,0:T(8,128)(2,1)}) %all-gather.3.cloned.1.call-update) | async-done | bytes 2097168 | tf_op jit(solution)/shard_map/all_gather | solution.py:37
  90.7 28.2 %while.46 = (s32[]{:T(128)}, f32[512]{0:T(512)S(1)}, f32[512]{0:T(512)S(1)}, s32[8192]{0:T(1024)S(1)}, bf16[8192,128]{1,0:T(8,128)(2,1)}, /*index=5*/bf16[512,12...) while((s32[]{:T(128)}, f32[512]{0:T(512)S(1)}, ...), condition=%wide.region_3.4_spmd.clone, body=%wide.region_0.3_spmd.clone.sunk | while | flops 70257160 | bytes 2407614 | solution.py:74
  118.9 50.1 %all-gather.5.cloned.1.call-done = bf16[8192,128]{1,0:T(8,128)(2,1)} async-done(((bf16[128,128]{1,0:T(8,128)(2,1)}), bf16[8192,128]{1,0:T(8,128)(2,1)}) %all-gather.5.cloned.1.call-update) | async-done | bytes 2097168 | tf_op jit(solution)/shard_map/all_gather | solution.py:38
  169.0 43.4 %while.47 = (s32[]{:T(128)}, f32[512]{0:T(512)S(1)}, s32[8192]{0:T(1024)S(1)}, bf16[8192,128]{1,0:T(8,128)(2,1)}, bf16[512,128]{1,0:T(8,128)(2,1)S(1)}, /*index=...) while((s32[]{:T(128)}, f32[512]{0:T(512)S(1)}, ...), condition=%wide.region_6.7_spmd.clone, body=%wide.region_4.6_spmd.clone.sunk | while | flops 136577536 | bytes 2647249 | solution.py:90
  169.1 1.4 fusion.98
  171.8 1.4 fusion.98
  174.5 1.4 fusion.98
  177.2 1.4 fusion.98
  180.0 1.4 fusion.98
  182.7 1.4 fusion.98
  185.4 1.4 fusion.98
  188.1 1.4 fusion.98
  190.8 1.4 fusion.98
  193.5 1.4 fusion.98
  196.3 1.4 fusion.98
  199.0 1.4 fusion.98
  201.7 1.4 fusion.98
  204.4 1.4 fusion.98
  207.1 1.4 fusion.98
  209.8 1.4 fusion.98
  212.4 4.2 broadcast_in_dim.81
  216.6 86.9 %while.48 = (s32[]{:T(128)}, f32[512,128]{1,0:T(8,128)S(1)}, f32[8192,256]{0,1:T(8,128)}, s32[8192]{0:T(1024)S(1)}, bf16[8192,128]{1,0:T(8,128)(2,1)}, /*index=5...) while((s32[]{:T(128)}, f32[512,128]{1,0:T(8,128)S(1)}, ...), condition=%wide.region_8.9_spmd.clone, body=%wide.region_7.8_spmd.clone.sunk | while | flops 338952192 | bytes 7752937 | solution.py:117
  216.7 1.4 fusion.110
  222.2 1.4 fusion.110
  227.6 1.4 fusion.110
  233.1 1.4 fusion.110
  238.5 1.4 fusion.110
  243.9 1.4 fusion.110
  249.3 1.4 fusion.110
  260.2 1.4 fusion.110
  265.6 1.4 fusion.110
  271.1 1.4 fusion.110
  276.5 1.4 fusion.110
  281.9 1.4 fusion.110
  287.4 1.4 fusion.110
  292.8 1.3 fusion.110
  303.6 150.1 %reduce-scatter.2.cloned.1.call-done = f32[128,256]{0,1:T(8,128)} async-done(((f32[8192,256]{0,1:T(8,128)}), f32[128,256]{0,1:T(8,128)}) %reduce-scatter.2.cloned.1.call-update) | async-done | bytes 131088 | tf_op jit(solution)/shard_map/reduce_scatter | solution.py:118
  454.7 11.9 %all_gather.11 = bf16[512,256]{0,1:T(8,128)(2,1)S(1)} all-gather(bf16[128,256]{0,1:T(8,128)(2,1)S(1)} %convert_element_type.54), channel_id=1, replica_groups=mesh['ctx'=64,'fsdp'=4] {'fsdp'}, dimensions={0}, use_global_device_ids=true | all-gather | bytes 327680 | tf_op jit(solution)/shard_map/all_gather | solution.py:125
  467.6 2.7 convolution_bitcast_fusion.1
  473.1 191.5 %all-reduce.3.cloned.1.call-done = f32[2048,512]{0,1:T(8,128)} async-done(((f32[2048,512]{0,1:T(8,128)}), f32[2048,512]{0,1:T(8,128)}) %all-reduce.3.cloned.1.call-update) | async-done | bytes 4194320 | tf_op jit(solution)/shard_map/psum | solution.py:137
  664.6 2.5 multiply_reduce_fusion
  667.1 10.5 %all-reduce = (f32[256]{0:T(256)S(1)}, f32[256]{0:T(256)S(1)}, f32[512]{0:T(512)S(1)}) all-reduce(f32[256]{0:T(256)S(1)} %get-tuple-element.720, f32[256]{0:T(256)S(1)} %get-tuple-element.721, f32[512]{0:T(512)S(1)} %multiply_reduce_fusion), channel_id=1, replica_groups=mesh['ctx'=64,'fsdp'=4] {'fsdp'}, use_global_device_ids=true, to_apply=%region_15.16 | all-reduce | flops 1024 | bytes 8192 | tf_op jit(solution)/shard_map/psum | solution.py:143
  677.6 2.5 broadcast_multiply_fusion
  680.2 1.7 fusion.54
  681.9 2.9 copy.33
  684.8 1.8 copy.34
  (331 shorter events, 125.1 us)
Async XLA Ops:
  7.2 460.4 %copy-start = (bf16[128,2048]{1,0:T(8,128)(2,1)S(1)}, bf16[128,2048]{1,0:T(8,128)(2,1)}, u32[]{:S(2)}) copy-start(bf16[128,2048]{1,0:T(8,128)(2,1)} %param.19) | copy-start | bytes 1572868
  7.2 83.5 %all-gather.3.cloned.1.call-start = ((), (), s32[]{:S(2)}) async-start(), calls=%async_computation.1 | async-start | bytes 2129920 | tf_op jit(solution)/shard_map/all_gather | solution.py:37
  8.7 160.3 %all-gather.5.cloned.1.call-start = ((), (), s32[]{:S(2)}) async-start(), calls=%async_computation.2 | async-start | bytes 2129920 | tf_op jit(solution)/shard_map/all_gather | solution.py:38
  10.1 443.6 %reduce-scatter.2.cloned.1.call-start = ((), (), s32[]{:S(2)}) async-start(), calls=%async_computation.3 | async-start | bytes 8519680 | tf_op jit(solution)/shard_map/reduce_scatter | solution.py:118
  303.6 361.0 %all-reduce.3.cloned.1.call-start = ((), (), s32[]{:S(2)}) async-start(), calls=%async_computation.4 | async-start | bytes 8388608 | tf_op jit(solution)/shard_map/psum | solution.py:137
  470.3 1.2 copy-start.1
  470.3 1.5 copy-start.2
Sparse Core Ops, SparseCore 0:
  11.3 79.3 all-gather.2
  94.0 74.9 all-gather.4
  303.7 150.0 reduce-scatter.1
  470.4 194.1 all-reduce.2
where the time goes:
time: 695 us; the launch traced here: 693 us
  waiting for transfers between devices  468 us (67%)
  matrix products  136 us (20%)
  other arithmetic  29 us (4%)
  blocking collectives  22.4 us (3%)
  local copies, waits for them, and re-layouts  21.9 us (3%)
  between operations  13.9 us (2%)
    psum x1, waiting for transfers between devices, local(): lax.psum(lax.dot_general(hidden, both_grads, contract_first, preferred_el...  192 us
    reduce_scatter x1, waiting for transfers between devices, local(): own_grads = lax.psum_scatter(terms, 'ctx', scatter_dimension=0, tiled=True)  150 us
    all_gather x1, waiting for transfers between devices, local(): lax.all_gather(own_keys, 'ctx', axis=0, tiled=True)  75.9 us
    dot_general x48, matrix products, scores_at(): lax.dot_general(query_rows, key_block, contract_last, preferred_element_t...  63.8 us
    all_gather x1, waiting for transfers between devices, local(): lax.all_gather(own_values, 'ctx', axis=0, tiled=True)  50.1 us
    dot_general x32, matrix products, probs_at(): lax.dot_general(grad_rows, value_block, contract_last, preferred_element_...  38.8 us
    dot_general x16, matrix products, full_step(): jnp.dot(slopes, key_block, preferred_element_type=jnp.float32)  20.5 us
  transfers between devices with their start and end apart: 4, of which 4 were waited for; matrix products, arithmetic and copies ran while one was open for 5% of the time, Pallas kernels for 0%

commit v1 on v0

--- a/solution.py
+++ b/solution.py
@@ -1,3 +1,4 @@
+import functools
 import math
 import jax
 import jax.numpy as jnp
@@ -10,6 +11,16 @@
 CLIP_RATE = 0.02
 EPSILON = 1e-06
 NEGATIVE = -1e30
+
+
+def draw_layers_all(inp, net_axis):
+    m_next = jax.lax.psum(1, net_axis)
+    row_out = jnp.stack(m_next * [inp])
+    res = jax.lax.all_to_all(row_out, net_axis, 0, 0)
+    return jnp.concatenate(res, axis=0)
+
+
+compute_packet_here = functools.partial(draw_layers_all, net_axis="ctx")
 
 
 def rows_by_head(block, heads, width):
@@ -35,7 +46,7 @@
     own_values = lax.dynamic_slice_in_dim(values, group * DH, DH, 1)
     all_keys, all_values = (
         lax.all_gather(own_keys, "ctx", axis=0, tiled=True),
-        lax.all_gather(own_values, "ctx", axis=0, tiled=True),
+        compute_packet_here(own_values),
     )
     offsets = jnp.arange(half, dtype=jnp.int32)
     stretches = jnp.stack([stretch_owner, 2 * ctx_count - 1 - stretch_owner], axis=1)

time: 695 us -> 647 us (0.931)
  waiting for transfers between devices: 468 us -> 410 us
  starting transfers between devices: 0.16 us -> 12.5 us
    all_gather x1 -> x0, waiting for transfers between devices: 50.1 us -> none  [local(): lax.all_gather(own_values, 'ctx', axis=0, tiled=True)]
    all_to_all x0 -> x1, starting transfers between devices: none -> 12.3 us  [draw_layers_all(): res = jax.lax.all_to_all(row_out, net_axis, 0, 0)]
    all_gather x1, waiting for transfers between devices: 75.9 us -> 67.9 us  [local(): lax.all_gather(own_keys, 'ctx', axis=0, tiled=True)]
  transfers between devices with their start and end apart: 4 -> 4, of which waited for: 4 -> 3; matrix products, arithmetic and copies ran while one was open for 5% -> 5% of each run, Pallas kernels for 0% -> 0%
where the time goes in v1:
time: 647 us; the launch traced here: 645 us
  waiting for transfers between devices  410 us (63%)
  matrix products  136 us (21%)
  other arithmetic  27 us (4%)
  blocking collectives  22.4 us (3%)
  local copies, waits for them, and re-layouts  21.3 us (3%)
  between operations  14 us (2%)
  starting transfers between devices  12.5 us (2%)
    psum x1, waiting for transfers between devices, local(): lax.psum(lax.dot_general(hidden, both_grads, contract_first, preferred_el...  192 us
    reduce_scatter x1, waiting for transfers between devices, local(): own_grads = lax.psum_scatter(terms, 'ctx', scatter_dimension=0, tiled=True)  150 us
    all_gather x1, waiting for transfers between devices, local(): lax.all_gather(own_keys, 'ctx', axis=0, tiled=True)  67.9 us
    dot_general x48, matrix products, scores_at(): lax.dot_general(query_rows, key_block, contract_last, preferred_element_t...  63.8 us
    dot_general x32, matrix products, probs_at(): lax.dot_general(grad_rows, value_block, contract_last, preferred_element_...  38.8 us
    dot_general x16, matrix products, full_step(): jnp.dot(slopes, key_block, preferred_element_type=jnp.float32)  20.6 us
    dynamic_update_slice x16, other arithmetic, full_step(): lax.dynamic_update_slice_in_dim(terms, key_terms(probs_b, slopes), start, 0)  13.7 us
  transfers between devices with their start and end apart: 4, of which 3 were waited for; matrix products, arithmetic and copies ran while one was open for 5% of the time, Pallas kernels for 0%

profile of v1, /device:TPU:2, one launch (start us, length us, event | category | flops | bytes accessed | tf_op | source)
XLA Modules:
  0.0 644.8 jit_solution(1977716977901615153)
XLA Ops:
  7.2 1.4 constant_dynamic-slice_fusion.1
  9.5 1.8 stack.11
  11.3 12.3 %all-to-all-start = ((bf16[64,128,128]{2,1,0:T(8,128)(2,1)}), bf16[64,128,128]{2,1,0:T(8,128)(2,1)}, u32[]{:S(2)}, u32[]{:S(2)}) async-start(bf16[64,128,128]{2,1,0:T(8,128)(2,1)} %stack.11), calls=%async_computation | async-start | bytes 4194304 | tf_op jit(solution)/shard_map/all_to_all | solution.py:19
  24.5 67.9 %all-gather.2.cloned.1.call-done = bf16[8192,128]{1,0:T(8,128)(2,1)} async-done(((bf16[128,128]{1,0:T(8,128)(2,1)}), bf16[8192,128]{1,0:T(8,128)(2,1)}) %all-gather.2.cloned.1.call-update) | async-done | bytes 2097168 | tf_op jit(solution)/shard_map/all_gather | solution.py:48
  92.5 28.2 %while.46 = (s32[]{:T(128)}, f32[512]{0:T(512)S(1)}, f32[512]{0:T(512)S(1)}, s32[8192]{0:T(1024)S(1)}, bf16[8192,128]{1,0:T(8,128)(2,1)}, /*index=5*/bf16[512,12...) while((s32[]{:T(128)}, f32[512]{0:T(512)S(1)}, ...), condition=%wide.region_3.4_spmd.clone, body=%wide.region_0.3_spmd.clone.sunk | while | flops 70257160 | bytes 2407614 | solution.py:85
  120.7 43.4 %while.47 = (s32[]{:T(128)}, f32[512]{0:T(512)S(1)}, s32[8192]{0:T(1024)S(1)}, bf16[8192,128]{1,0:T(8,128)(2,1)}, bf16[512,128]{1,0:T(8,128)(2,1)S(1)}, /*index=...) while((s32[]{:T(128)}, f32[512]{0:T(512)S(1)}, ...), condition=%wide.region_6.7_spmd.clone, body=%wide.region_4.6_spmd.clone.sunk | while | flops 136577536 | bytes 2647249 | solution.py:101
  123.5 1.4 fusion.98
  126.2 1.4 fusion.98
  128.9 1.4 fusion.98
  131.6 1.4 fusion.98
  134.3 1.4 fusion.98
  137.1 1.4 fusion.98
  139.8 1.4 fusion.98
  142.5 1.4 fusion.98
  145.2 1.4 fusion.98
  147.9 1.4 fusion.98
  150.6 1.4 fusion.98
  153.3 1.4 fusion.98
  156.0 1.4 fusion.98
  158.8 1.4 fusion.98
  161.5 1.4 fusion.98
  164.1 4.2 broadcast_in_dim.81
  168.3 87.0 %while.48 = (s32[]{:T(128)}, f32[512,128]{1,0:T(8,128)S(1)}, f32[8192,256]{0,1:T(8,128)}, s32[8192]{0:T(1024)S(1)}, bf16[8192,128]{1,0:T(8,128)(2,1)}, /*index=5...) while((s32[]{:T(128)}, f32[512,128]{1,0:T(8,128)S(1)}, ...), condition=%wide.region_8.9_spmd.clone, body=%wide.region_7.8_spmd.clone.sunk | while | flops 338952192 | bytes 7752937 | solution.py:128
  168.3 1.4 fusion.110
  173.8 1.4 fusion.110
  179.3 1.4 fusion.110
  184.7 1.4 fusion.110
  190.2 1.4 fusion.110
  195.6 1.4 fusion.110
  201.0 1.4 fusion.110
  206.5 1.4 fusion.110
  211.9 1.4 fusion.110
  217.3 1.4 fusion.110
  222.8 1.4 fusion.110
  228.2 1.4 fusion.110
  233.7 1.4 fusion.110
  244.5 1.4 fusion.110
  249.9 1.4 fusion.110
  255.4 150.1 %reduce-scatter.2.cloned.1.call-done = f32[128,256]{0,1:T(8,128)} async-done(((f32[8192,256]{0,1:T(8,128)}), f32[128,256]{0,1:T(8,128)}) %reduce-scatter.2.cloned.1.call-update) | async-done | bytes 131088 | tf_op jit(solution)/shard_map/reduce_scatter | solution.py:129
  406.4 11.9 %all_gather.7 = bf16[512,256]{0,1:T(8,128)(2,1)S(1)} all-gather(bf16[128,256]{0,1:T(8,128)(2,1)S(1)} %convert_element_type.54), channel_id=1, replica_groups=mesh['ctx'=64,'fsdp'=4] {'fsdp'}, dimensions={0}, use_global_device_ids=true | all-gather | bytes 327680 | tf_op jit(solution)/shard_map/all_gather | solution.py:136
  419.3 2.7 convolution_bitcast_fusion.1
  424.8 191.5 %all-reduce.3.cloned.1.call-done = f32[2048,512]{0,1:T(8,128)} async-done(((f32[2048,512]{0,1:T(8,128)}), f32[2048,512]{0,1:T(8,128)}) %all-reduce.3.cloned.1.call-update) | async-done | bytes 4194320 | tf_op jit(solution)/shard_map/psum | solution.py:148
  616.3 2.5 multiply_reduce_fusion
  618.8 10.5 %all-reduce = (f32[256]{0:T(256)S(1)}, f32[256]{0:T(256)S(1)}, f32[512]{0:T(512)S(1)}) all-reduce(f32[256]{0:T(256)S(1)} %get-tuple-element.720, f32[256]{0:T(256)S(1)} %get-tuple-element.721, f32[512]{0:T(512)S(1)} %multiply_reduce_fusion), channel_id=1, replica_groups=mesh['ctx'=64,'fsdp'=4] {'fsdp'}, use_global_device_ids=true, to_apply=%region_15.16 | all-reduce | flops 1024 | bytes 8192 | tf_op jit(solution)/shard_map/psum | solution.py:154
  629.3 2.5 broadcast_multiply_fusion
  631.9 1.7 fusion.54
  633.6 2.9 copy.33
  636.4 1.8 copy.34
  (339 shorter events, 122.1 us)
Async XLA Ops:
  7.2 412.1 %copy-start = (bf16[128,2048]{1,0:T(8,128)(2,1)S(1)}, bf16[128,2048]{1,0:T(8,128)(2,1)}, u32[]{:S(2)}) copy-start(bf16[128,2048]{1,0:T(8,128)(2,1)} %param.19) | copy-start | bytes 1572868
  7.2 85.3 %all-gather.2.cloned.1.call-start = ((), (), s32[]{:S(2)}) async-start(), calls=%async_computation.2 | async-start | bytes 2129920 | tf_op jit(solution)/shard_map/all_gather | solution.py:48
  11.3 12.5 %copy-start.5 = (s32[64]{0:T(128)S(1)}, s32[64]{0:T(128)}, u32[]{:S(2)}) copy-start(s32[64]{0:T(128)} %param.22) | copy-start | bytes 772
  11.3 13.2 %copy-start.6 = (s32[128]{0:T(128)S(1)}, s32[128]{0:T(128)}, u32[]{:S(2)}) copy-start(s32[128]{0:T(128)} %param.23) | copy-start | bytes 1540
  11.3 13.2 %copy-start.3 = (bf16[128,512]{1,0:T(8,128)(2,1)S(1)}, bf16[128,512]{1,0:T(8,128)(2,1)}, u32[]{:S(2)}) copy-start(bf16[128,512]{1,0:T(8,128)(2,1)} %param.15) | copy-start | bytes 393220
  11.3 13.2 %copy-start.4 = (bf16[128,512]{1,0:T(8,128)(2,1)S(1)}, bf16[128,512]{1,0:T(8,128)(2,1)}, u32[]{:S(2)}) copy-start(bf16[128,512]{1,0:T(8,128)(2,1)} %param.18) | copy-start | bytes 393220
  11.3 109.4 %all-to-all-start = ((bf16[64,128,128]{2,1,0:T(8,128)(2,1)}), bf16[64,128,128]{2,1,0:T(8,128)(2,1)}, u32[]{:S(2)}, u32[]{:S(2)}) async-start(bf16[64,128,128]{2,1,0:T(8,128)(2,1)} %stack.11), calls=%async_computation | async-start | bytes 4194304 | tf_op jit(solution)/shard_map/all_to_all | solution.py:19
  23.7 381.8 %reduce-scatter.2.cloned.1.call-start = ((), (), s32[]{:S(2)}) async-start(), calls=%async_computation.3 | async-start | bytes 8519680 | tf_op jit(solution)/shard_map/reduce_scatter | solution.py:129
  255.3 361.0 %all-reduce.3.cloned.1.call-start = ((), (), s32[]{:S(2)}) async-start(), calls=%async_computation.4 | async-start | bytes 8388608 | tf_op jit(solution)/shard_map/psum | solution.py:148
  422.0 1.2 copy-start.1
  422.0 1.5 copy-start.2
Sparse Core Ops, SparseCore 0:
  11.3 81.0 all-gather.1
  255.5 149.9 reduce-scatter.1
  422.1 194.1 all-reduce.2
